TPU v7x, 256 devices: a whole 4x4x8 slice. The times are simulated.
256 devices in a mesh: src: 64 (over z, y_hi, x), row: 4 (over y_lo, core).
Axes of the slice: x: 4, y: 4 (y_hi: 2, y_lo: 2; y = y_hi * 2 + y_lo), z: 8, core: 2. Of those that a mesh axis runs over, the one named last changes fastest.
Arguments:
- factor: float32 [10240, 1024], P(('row', 'src')), as said below
- right_side: float32 [10240, 32768], P('row', 'src'), may hold values from -6 to 6
Outputs:
- advanced: float32 [10240, 32768], P('row', 'src')
Inputs may be any that keep to these rules, and one draw needn't show every extreme that they name: factor is zero where its column index exceeds its row index, and its entries where the two are equal lie between 1 and 2.
All inputs are finite; a program needn't handle non-finite values.
Results may differ from a plain program's by a relative error of at most 0.0001.
Values sent between devices are 32-bit elements; how exact they have to be, the bound alone decides.
A program may use at most 64 MiB of HBM per device.

v0:
```python
import jax
import jax.numpy as jnp
from jax import lax
from jax.sharding import PartitionSpec as P


def broadcast(block, axis, holder):
    block = jnp.where(lax.axis_index(axis) == holder, block, jnp.zeros_like(block))
    return lax.psum(block, axis)


def spread_solved(solved):
    return broadcast(solved, "row", 0)


def advance_panel(panel, current, offset, width, start_row):
    diag_block = panel[offset : offset + width]
    solved = lax.linalg.triangular_solve(
        diag_block, current[offset : offset + width], left_side=True, lower=True
    )
    solved = spread_solved(solved)
    product = jnp.dot(
        panel, solved, preferred_element_type=jnp.float32, precision=lax.Precision.HIGHEST
    )
    row_ids = start_row + jnp.arange(current.shape[0], dtype=jnp.int32)[:, None]
    updated = jnp.where(row_ids >= offset + width, current - product, current)
    holder = row_ids[offset : offset + width] < offset + width
    placed = jnp.where(holder, solved, updated[offset : offset + width])
    return lax.dynamic_update_slice_in_dim(updated, placed, offset, 0)


def local(factor, right_side):
    width = factor.shape[1] // 2
    local_rows = right_side.shape[0]
    start_row = lax.axis_index("row") * local_rows
    current = right_side
    gathered = lax.all_gather(factor, "src", axis=0, tiled=True)
    first_panel = gathered[:, :width]
    second_panel = gathered[:, width:]
    current = advance_panel(first_panel, current, 0, width, start_row)
    current = advance_panel(second_panel, current, width, width, start_row)
    return current


def solution(mesh):
    placed = (P(("row", "src"), None), P("row", "src"))
    return jax.shard_map(
        local, mesh=mesh, in_specs=placed, out_specs=P("row", "src"), check_vma=False
    )
```

profile of v0, /device:TPU:1, one launch (start us, length us, event | category | flops | bytes accessed | tf_op | source)
XLA Modules:
  0.0 364.1 jit_solution(3990240733775104262)
XLA Ops:
  6.5 0.7 all-gather.2.cloned.1.call-update
  7.4 165.0 %all-gather.2.cloned.1.call-done = f32[2560,1024]{1,0:T(8,128)} async-done(((f32[40,1024]{1,0:T(8,128)}), f32[2560,1024]{1,0:T(8,128)}) %all-gather.2.cloned.1.call-update) | async-done | bytes 10485776 | tf_op jit(solution)/shard_map/all_gather | solution.py:37
  172.4 1.8 slice_select_fusion.1
  174.2 8.1 %while.4 = (s32[]{:T(128)}, f32[512,512]{1,0:T(8,128)S(1)}, s32[4,2]{0,1:T(2,128)S(1)}, f32[4,128,128]{2,1,0:T(8,128)S(1)}, s32[]{:T(128)}) while((s32[]{:T(128)}, f32[512,512]{1,0:T(8,128)S(1)}, s32[4,2]{0,1:T(2,128)S(1)}, f32[4,128,128]{2,1,0:T(8,128)S(1)}, s32[]{:T(128)}) %tuple.37), condition=%wide.while_cond, body=%wide.while_body.sunk | while | flops 2 | bytes 131181 | solution.py:18
  174.3 0.6 fusion.62
  174.9 1.3 bitcast_dynamic-update-slice_fusion.4
  177.0 1.3 bitcast_dynamic-update-slice_fusion.4
  178.4 0.6 fusion.62
  179.0 1.3 bitcast_dynamic-update-slice_fusion.4
  181.0 1.3 bitcast_dynamic-update-slice_fusion.4
  182.4 39.3 %custom-call.4 = f32[4,128,128]{1,2,0:T(8,128)S(1)} custom-call(f32[4,128,128]{2,1,0:T(8,128)S(1)} %get-tuple-element.20), custom_call_target="InvertDiagBlocksLowerTriangular" | custom-call | tf_op jit(solution)/shard_map/triangular_solve/custom-call.1 | solution.py:18
  221.7 1.4 fusion.28
  223.1 1.3 convolution_subtract_fusion.3
  224.8 1.4 convolution_subtract_fusion.2
  226.6 1.6 convolution_subtract_fusion.5
  228.7 1.1 maximum_select_fusion
  230.0 8.4 %while.5 = (s32[]{:T(128)}, f32[512,512]{1,0:T(8,128)S(1)}, s32[4,2]{0,1:T(2,128)S(1)}, f32[4,128,128]{2,1,0:T(8,128)S(1)}, s32[]{:T(128)}) while((s32[]{:T(128)}, f32[512,512]{1,0:T(8,128)S(1)}, s32[4,2]{0,1:T(2,128)S(1)}, f32[4,128,128]{2,1,0:T(8,128)S(1)}, s32[]{:T(128)}) %tuple.49), condition=%wide.while_cond.clone, body=%wide.while_body.clone.sunk | while | flops 2 | bytes 131181 | solution.py:18
  230.1 0.6 fusion.63
  230.7 1.4 bitcast_dynamic-update-slice_fusion.5
  232.2 0.6 fusion.63
  232.8 1.4 bitcast_dynamic-update-slice_fusion.5
  234.3 0.6 fusion.63
  234.9 1.4 bitcast_dynamic-update-slice_fusion.5
  236.4 0.6 fusion.63
  237.0 1.4 bitcast_dynamic-update-slice_fusion.5
  238.4 39.3 %custom-call.5 = f32[4,128,128]{1,2,0:T(8,128)S(1)} custom-call(f32[4,128,128]{2,1,0:T(8,128)S(1)} %get-tuple-element.21), custom_call_target="InvertDiagBlocksLowerTriangular" | custom-call | tf_op jit(solution)/shard_map/triangular_solve/custom-call.1 | solution.py:18
  277.8 12.3 %subtract_select_fusion.1 = f32[2560,512]{1,0:T(8,128)S(1)} fusion(f32[2560,512]{1,0:T(8,128)} %param.5, f32[512,512]{1,0:T(8,128)} %all-reduce.3.cloned.1.call-done, f32[2560,1024]{1,0:T(8,128)} %all-gather.2.cloned.1.call-done, pred[2560]{0:T(1024)(128)(4,1)S(1)} %fusion.42), kind=kOutput, calls=%fused_computation.5 | convolution fusion | flops 8055685120 | bytes 16779776 | tf_op jit(solution)/shard_map/dot_general | solution.py:22
  292.7 0.6 convolution_subtract_fusion.4
  293.7 1.1 maximum_select_fusion.1
  294.9 45.7 %all-reduce.5.cloned.1.call-done = f32[512,512]{1,0:T(8,128)} async-done(((f32[512,512]{1,0:T(8,128)}), f32[512,512]{1,0:T(8,128)}) %all-reduce.5.cloned.1.call-update) | async-done | bytes 1048592 | tf_op jit(solution)/shard_map/psum | solution.py:9
  340.6 14.7 %subtract_select_fusion = f32[2560,512]{1,0:T(8,128)} fusion(f32[2560,512]{1,0:T(8,128)} %copy-done, f32[512,512]{1,0:T(8,128)} %all-reduce.5.cloned.1.call-done, f32[2560,1024]{1,0:T(8,128)} %all-gather.2.cloned.1.call-done, pred[2560]{0:T(1024)(128)(4,1)S(1)} %fusion.43), kind=kOutput, calls=%fused_computation.4 | convolution fusion | flops 8055685120 | bytes 16779776 | tf_op jit(solution)/shard_map/dot_general | solution.py:22
  355.3 2.4 fusion.8
  (40 shorter events, 6.4 us)
Async XLA Ops:
  6.5 165.9 %all-gather.2.cloned.1.call-start = ((), (), s32[]{:S(2)}) async-start(), calls=%async_computation | async-start | bytes 10649600 | tf_op jit(solution)/shard_map/all_gather | solution.py:37
  7.3 270.5 %all-reduce.3.cloned.1.call-start = ((), (), s32[]{:S(2)}) async-start(), calls=%async_computation.1 | async-start | bytes 2097152 | tf_op jit(solution)/shard_map/psum | solution.py:9
  229.7 110.8 %all-reduce.5.cloned.1.call-start = ((), (), s32[]{:S(2)}) async-start(), calls=%async_computation.2 | async-start | bytes 2097152 | tf_op jit(solution)/shard_map/psum | solution.py:9
  277.8 12.3 %copy-start.1 = (f32[512,512]{1,0:T(8,128)S(1)}, f32[512,512]{1,0:T(8,128)}, u32[]{:S(2)}) copy-start(f32[512,512]{1,0:T(8,128)} %all-reduce.3.cloned.1.call-done) | copy-start | bytes 3145732
  290.3 2.4 copy-start
  340.6 14.7 %copy-start.2 = (f32[512,512]{1,0:T(8,128)S(1)}, f32[512,512]{1,0:T(8,128)}, u32[]{:S(2)}) copy-start(f32[512,512]{1,0:T(8,128)} %all-reduce.5.cloned.1.call-done) | copy-start | bytes 3145732
Sparse Core Ops, SparseCore 0:
  10.9 161.4 all-gather.1
  229.9 44.6 all-reduce.2
  295.0 45.5 all-reduce.4
where the time goes:
time: 365 us; the launch traced here: 364 us
  waiting for transfers between devices  211 us (58%)
  other arithmetic  85.2 us (23%)
  matrix products  37 us (10%)
  local copies, waits for them, and re-layouts  16.6 us (5%)
  between operations  13.4 us (4%)
    all_gather x1, waiting for transfers between devices, local(): gathered = lax.all_gather(factor, 'src', axis=0, tiled=True)  165 us
    another operation x4, other arithmetic, advance_panel(): lax.linalg.triangular_solve(diag_block, current[offset:offset + width], l...  80.4 us
    psum x2, waiting for transfers between devices, broadcast(): return lax.psum(block, axis)  45.7 us
    dot_general x2, matrix products, advance_panel(): jnp.dot(panel, solved, preferred_element_type=jnp.float32, precision=lax....  27 us
    another operation x26, local copies, waits for them, and re-layouts, advance_panel(): lax.linalg.triangular_solve(diag_block, current[offset:offset + width], l...  16.4 us
    another operation x14, matrix products, advance_panel(): lax.linalg.triangular_solve(diag_block, current[offset:offset + width], l...  10 us
  transfers between devices with their start and end apart: 3, of which 2 were waited for; matrix products, arithmetic and copies ran while one was open for 13% of the time, Pallas kernels for 0%

commit v1 on v0

--- a/solution.py
+++ b/solution.py
@@ -1,7 +1,133 @@
+import heapq
+
 import jax
 import jax.numpy as jnp
 from jax import lax
+from jax.experimental import pallas as pl
+from jax.experimental.pallas import tpu as pltpu
 from jax.sharding import PartitionSpec as P
+
+MESH = pl.DeviceIdType.MESH
+
+SB = 4096 * 8
+def plan(A=2, NB=5, rate=46.5e3, lat=1.7, ylat=2.6, yrate=23e3, verbose=False):
+    szA, szB = A * SB, (NB - A) * SB
+    size = {"Y": NB * SB, "B1": szB, "B3": szB, "A1": szA, "A3": 4 * szA}
+    nexthop = []
+    free = {k: 0.0 for k in ("x+", "x-", "z+", "z-", "y")}
+    busy = dict.fromkeys(free, 0.0)
+    heap, order, cnt = [], [], 0
+    sends = []
+    def send(t, link, tag):
+        nonlocal cnt
+        r = yrate if link == "y" else rate
+        s = max(t, free[link]); e = s + size[tag[0]] / r
+        free[link] = e; busy[link] += size[tag[0]] / r
+        sends.append((t, s, link, tag))
+        heapq.heappush(heap, (e + (ylat if link == "y" else lat), cnt, link, tag)); cnt += 1
+        order.append(("send", link, tag))
+    def own(t, dh):
+        for l in ("z+", "z-"): send(t, l, ("B1", 0, dh, 0))
+        for l in ("x+", "x-"): send(t, l, ("A1", 0, dh, 0))
+        for l in ("x+", "x-"): send(t, l, ("B3", 0, dh, 0))
+    send(0, "y", ("Y", 0, 0, 0)); own(0, 0)
+    got = {0: 0, 1: 0}
+    T = 0
+    arr = []
+    while heap:
+        t, _, link, tag = heapq.heappop(heap)
+        k, dz, dh, dx = tag
+        s = {"+": 1, "-": -1}.get(link[-1], 0)
+        order.append(("recv", link, tag)); T = t; arr.append((t, link, tag))
+        if k == "Y": own(t, 1); continue
+        if link[0] == "x": dx -= s
+        else: dz -= s
+        if k in ("B1", "A3"):
+            d = abs(dz)
+            if d + 1 <= 3 or (d + 1 == 4 and (dh == 0) == (s == 1)):
+                send(t, link, (k, dz, dh, dx))
+            if k == "B1":
+                for l in ("x+", "x-"): send(t, l, ("B3", dz, dh, 0))
+        else:
+            if abs(dx) == 1 and (dh == 0) == (s == 1):
+                send(t, link, (k, dz, dh, dx))
+            if k == "A1":
+                got[dh] += 1
+                if got[dh] == 3:
+                    for l in ("z+", "z-"): send(t, l, ("A3", 0, dh, 0))
+    if verbose:
+        print("end", T, busy, "nsend", len(sends))
+        for a in arr: print(a)
+    return order, T
+
+
+def make(A=2, NB=5, order=None, space=pl.ANY):
+    if order is None:
+        order, _ = plan(A, NB)
+    RA = 8 * A
+    RN = 8 * NB
+    sends = [o for o in order if o[0] == "send"]
+    idx = {(o[1], o[2]): i for i, o in enumerate(sends)}
+    n = len(sends)
+    def kernel(f_ref, g_ref, ssem, rsem, lsem):
+        src = lax.axis_index("src"); row = lax.axis_index("row")
+        z = src // 8; h = lax.rem(src // 4, 2); x = lax.rem(src, 4)
+        def dev(dz=0, dh=0, dx=0):
+            zz = lax.rem(z + dz + 8, 8); xx = lax.rem(x + dx + 4, 4)
+            hh = h if not dh else 1 - h
+            return (zz * 8 + hh * 4 + xx, row)
+        nb = {"x+": dev(dx=1), "x-": dev(dx=-1), "z+": dev(dz=1), "z-": dev(dz=-1), "y": dev(dh=1)}
+        bar = pltpu.get_barrier_semaphore()
+        for k in nb.values():
+            pl.semaphore_signal(bar, inc=1, device_id=k, device_id_type=MESH)
+        loc = pltpu.make_async_copy(f_ref, g_ref.at[z, h, x], lsem)
+        loc.start()
+        pl.semaphore_wait(bar, len(nb))
+        def ref(tag, own=True):
+            k, dz, dh, dx = tag
+            rows = {"Y": (0, RN), "B1": (RA, RN), "B3": (RA, RN), "A1": (0, RA), "A3": (0, RA)}[k]
+            rs = pl.ds(rows[0], rows[1] - rows[0])
+            if own and dz == 0 and dh == 0 and dx == 0 and k != "A3":
+                s = f_ref.at[rs]
+            else:
+                s = None
+            zz = lax.rem(z + dz + 8, 8); hh = h if not dh else 1 - h
+            if k == "A3":
+                g = g_ref.at[zz, hh, :, rs]
+            else:
+                g = g_ref.at[zz, hh, lax.rem(x + dx + 4, 4), rs]
+            return (s if s is not None else g), g
+        def desc(link, tag, shift):
+            k, dz, dh, dx = tag
+            if shift:
+                s = {"+": 1, "-": -1}.get(link[-1], 0)
+                t = (k, dz - s if link[0] == "z" else dz, 1 - dh if link == "y" else dh, dx - s if link[0] == "x" else dx)
+                _, a = ref(t, own=False)
+                b = a
+            else:
+                a, b = ref(tag)
+            i = idx[(link, tag)]
+            return pltpu.make_async_remote_copy(src_ref=a, dst_ref=b, send_sem=ssem.at[i], recv_sem=rsem.at[i], device_id=nb[link], device_id_type=MESH)
+        waited = False
+        for op, link, tag in order:
+            if op == "send":
+                if tag[0] == "A3" and not waited:
+                    loc.wait(); waited = True
+                desc(link, tag, False).start()
+            else:
+                desc(link, tag, True).wait_recv()
+        for _, link, tag in sends:
+            desc(link, tag, False).wait_send()
+    def gather(f):
+        return pl.pallas_call(
+            kernel,
+            out_shape=jax.ShapeDtypeStruct((8, 2, 4, RN, 1024), jnp.float32),
+            in_specs=[pl.BlockSpec(memory_space=pltpu.VMEM)],
+            out_specs=pl.BlockSpec(memory_space=space),
+            scratch_shapes=[pltpu.SemaphoreType.DMA((n,)), pltpu.SemaphoreType.DMA((n,)), pltpu.SemaphoreType.DMA],
+            compiler_params=pltpu.CompilerParams(collective_id=0, has_side_effects=True),
+        )(f)
+    return gather
 
 
 def broadcast(block, axis, holder):
@@ -34,7 +160,7 @@
     local_rows = right_side.shape[0]
     start_row = lax.axis_index("row") * local_rows
     current = right_side
-    gathered = lax.all_gather(factor, "src", axis=0, tiled=True)
+    gathered = make()(factor).reshape(local_rows, factor.shape[1])
     first_panel = gathered[:, :width]
     second_panel = gathered[:, width:]
     current = advance_panel(first_panel, current, 0, width, start_row)

time: 365 us -> 270 us (0.74)
  waiting for transfers between devices: 211 us -> 48.7 us
  Pallas kernels: 0 us -> 68.4 us
    all_gather x1 -> x0, waiting for transfers between devices: 165 us -> none  [local(): gathered = lax.all_gather(factor, 'src', axis=0, tiled=True)]
    pallas_call x0 -> x1, Pallas kernels: none -> 68.4 us  [gather(): pl.pallas_call(kernel, out_shape=jax.ShapeDtypeStruct((8, 2, 4, RN, 1024)...]
  transfers between devices with their start and end apart: 3 -> 2, of which waited for: 2 -> 2; matrix products, arithmetic and copies ran while one was open for 13% -> 17% of each run, Pallas kernels for 0% -> 0%
where the time goes in v1:
time: 270 us; the launch traced here: 269 us
  other arithmetic  85.2 us (32%)
  Pallas kernels  68.4 us (25%)
  waiting for transfers between devices  48.7 us (18%)
  matrix products  38.2 us (14%)
  local copies, waits for them, and re-layouts  15 us (6%)
  between operations  13.7 us (5%)
    another operation x4, other arithmetic, advance_panel(): lax.linalg.triangular_solve(diag_block, current[offset:offset + width], l...  80.4 us
    pallas_call x1, Pallas kernels, gather(): pl.pallas_call(kernel, out_shape=jax.ShapeDtypeStruct((8, 2, 4, RN, 1024)...  68.4 us
    psum x2, waiting for transfers between devices, broadcast(): return lax.psum(block, axis)  48.7 us
    dot_general x2, matrix products, advance_panel(): jnp.dot(panel, solved, preferred_element_type=jnp.float32, precision=lax....  28.2 us
    another operation x26, local copies, waits for them, and re-layouts, advance_panel(): lax.linalg.triangular_solve(diag_block, current[offset:offset + width], l...  14.7 us
    another operation x14, matrix products, advance_panel(): lax.linalg.triangular_solve(diag_block, current[offset:offset + width], l...  10 us
  transfers between devices with their start and end apart: 2, of which 2 were waited for; matrix products, arithmetic and copies ran while one was open for 17% of the time, Pallas kernels for 0%

profile of v1, /device:TPU:1, one launch (start us, length us, event | category | flops | bytes accessed | tf_op | source)
XLA Modules:
  0.0 269.5 jit_solution(5913611717432645719)
XLA Ops:
  6.5 68.4 %shard_map.28 = f32[8,2,4,40,1024]{4,3,2,1,0:T(8,128)} custom-call(f32[40,1024]{1,0:T(8,128)} %f_ref.1), custom_call_target="tpu_custom_call" | custom-call | tf_op jit(solution)/shard_map/pallas_call | solution.py:122
  74.9 1.8 slice_select_fusion.1
  76.8 7.7 %while.4 = (s32[]{:T(128)}, f32[512,512]{1,0:T(8,128)S(1)}, s32[4,2]{0,1:T(2,128)S(1)}, f32[4,128,128]{2,1,0:T(8,128)S(1)}, s32[]{:T(128)}) while((s32[]{:T(128)}, f32[512,512]{1,0:T(8,128)S(1)}, s32[4,2]{0,1:T(2,128)S(1)}, f32[4,128,128]{2,1,0:T(8,128)S(1)}, s32[]{:T(128)}) %tuple.37), condition=%wide.while_cond, body=%wide.while_body.sunk | while | flops 2 | bytes 131181 | solution.py:144
  76.9 0.5 fusion.62
  77.4 1.3 bitcast_dynamic-update-slice_fusion.4
  78.8 0.5 fusion.62
  79.3 1.3 bitcast_dynamic-update-slice_fusion.4
  80.7 0.5 fusion.62
  81.3 1.3 bitcast_dynamic-update-slice_fusion.4
  82.6 0.5 fusion.62
  83.2 1.3 bitcast_dynamic-update-slice_fusion.4
  84.5 39.3 %custom-call.4 = f32[4,128,128]{1,2,0:T(8,128)S(1)} custom-call(f32[4,128,128]{2,1,0:T(8,128)S(1)} %get-tuple-element.20), custom_call_target="InvertDiagBlocksLowerTriangular" | custom-call | tf_op jit(solution)/shard_map/triangular_solve/custom-call.1 | solution.py:144
  123.8 1.4 fusion.28
  125.2 1.3 convolution_subtract_fusion.3
  126.9 1.4 convolution_subtract_fusion.2
  128.8 1.6 convolution_subtract_fusion.5
  130.8 1.1 maximum_select_fusion
  132.1 7.2 %while.5 = (s32[]{:T(128)}, f32[512,512]{1,0:T(8,128)S(1)}, s32[4,2]{0,1:T(2,128)S(1)}, f32[4,128,128]{2,1,0:T(8,128)S(1)}, s32[]{:T(128)}) while((s32[]{:T(128)}, f32[512,512]{1,0:T(8,128)S(1)}, s32[4,2]{0,1:T(2,128)S(1)}, f32[4,128,128]{2,1,0:T(8,128)S(1)}, s32[]{:T(128)}) %tuple.47), condition=%wide.while_cond.clone, body=%wide.while_body.clone.sunk | while | flops 2 | bytes 131181 | solution.py:144
  132.2 0.5 fusion.63
  132.7 1.2 bitcast_dynamic-update-slice_fusion.5
  134.5 1.2 bitcast_dynamic-update-slice_fusion.5
  136.3 1.2 bitcast_dynamic-update-slice_fusion.5
  137.6 0.5 fusion.63
  138.1 1.2 bitcast_dynamic-update-slice_fusion.5
  139.3 39.3 %custom-call.5 = f32[4,128,128]{1,2,0:T(8,128)S(1)} custom-call(f32[4,128,128]{2,1,0:T(8,128)S(1)} %get-tuple-element.21), custom_call_target="InvertDiagBlocksLowerTriangular" | custom-call | tf_op jit(solution)/shard_map/triangular_solve/custom-call.1 | solution.py:144
  178.7 0.8 all-reduce.3.cloned.1.call-done
  179.5 13.5 %subtract_select_fusion.1 = f32[2560,512]{1,0:T(8,128)S(1)} fusion(f32[2560,512]{1,0:T(8,128)} %param.5, f32[512,512]{1,0:T(8,128)} %all-reduce.3.cloned.1.call-done, f32[2560,1024]{1,0:T(8,128)} %bitcast.60, pred[2560]{0:T(1024)(128)(4,1)S(1)} %fusion.42), kind=kOutput, calls=%fused_computation.5 | convolution fusion | flops 8055685120 | bytes 16779776 | tf_op jit(solution)/shard_map/dot_general | solution.py:148
  195.6 0.6 convolution_subtract_fusion.4
  196.7 1.1 maximum_select_fusion.1
  197.8 47.8 %all-reduce.5.cloned.1.call-done = f32[512,512]{1,0:T(8,128)} async-done(((f32[512,512]{1,0:T(8,128)}), f32[512,512]{1,0:T(8,128)}) %all-reduce.5.cloned.1.call-update) | async-done | bytes 1048592 | tf_op jit(solution)/shard_map/psum | solution.py:135
  245.6 14.6 %subtract_select_fusion = f32[2560,512]{1,0:T(8,128)} fusion(f32[2560,512]{1,0:T(8,128)} %copy-done, f32[512,512]{1,0:T(8,128)} %all-reduce.5.cloned.1.call-done, f32[2560,1024]{1,0:T(8,128)} %bitcast.61, pred[2560]{0:T(1024)(128)(4,1)S(1)} %fusion.43), kind=kOutput, calls=%fused_computation.4 | convolution fusion | flops 8055685120 | bytes 16779776 | tf_op jit(solution)/shard_map/dot_general | solution.py:148
  260.3 2.4 fusion.8
  (38 shorter events, 6.1 us)
Async XLA Ops:
  6.5 173.0 %all-reduce.3.cloned.1.call-start = ((), (), s32[]{:S(2)}) async-start(), calls=%async_computation | async-start | bytes 2097152 | tf_op jit(solution)/shard_map/psum | solution.py:135
  131.9 113.8 %all-reduce.5.cloned.1.call-start = ((), (), s32[]{:S(2)}) async-start(), calls=%async_computation.1 | async-start | bytes 2097152 | tf_op jit(solution)/shard_map/psum | solution.py:135
  179.5 13.5 %copy-start.1 = (f32[512,512]{1,0:T(8,128)S(1)}, f32[512,512]{1,0:T(8,128)}, u32[]{:S(2)}) copy-start(f32[512,512]{1,0:T(8,128)} %all-reduce.3.cloned.1.call-done) | copy-start | bytes 3145732
  193.3 2.4 copy-start
  245.6 14.7 %copy-start.2 = (f32[512,512]{1,0:T(8,128)S(1)}, f32[512,512]{1,0:T(8,128)}, u32[]{:S(2)}) copy-start(f32[512,512]{1,0:T(8,128)} %all-reduce.5.cloned.1.call-done) | copy-start | bytes 3145732
Sparse Core Ops, SparseCore 0:
  132.0 47.4 all-reduce.2
  197.9 47.6 all-reduce.4

commit v2 on v0

v2 whole, which is shorter than its diff:
```python
import heapq

import jax
import jax.numpy as jnp
from jax import lax
from jax.experimental import pallas as pl
from jax.experimental.pallas import tpu as pltpu
from jax.sharding import PartitionSpec as P

MESH = pl.DeviceIdType.MESH
NX, NH, NZ = 4, 2, 8
PIECE = 40
COLS = 1024
WIDTH = 512
BLK = 128
STEPS = COLS // BLK
RATE = {"x+": 46e3, "x-": 46e3, "z+": 75e3, "z-": 75e3, "y": 23e3}


def plan(rows_a, latency=1.7):
    size = {"Y": PIECE, "B1": PIECE - rows_a, "B3": PIECE - rows_a, "A1": rows_a, "A3": 4 * rows_a}
    free = dict.fromkeys(RATE, 0.0)
    heap, order = [], []

    def send(t, link, tag):
        end = max(t, free[link]) + size[tag[0]] * 4096 / RATE[link]
        free[link] = end
        heapq.heappush(heap, (end + latency, len(order), link, tag))
        order.append(("send", link, tag))

    def own(t, dh):
        for link in ("x+", "x-"):
            send(t, link, ("A1", 0, dh, 0))
        for link in ("z+", "z-"):
            send(t, link, ("B1", 0, dh, 0))
        for link in ("x+", "x-"):
            send(t, link, ("B3", 0, dh, 0))

    send(0, "y", ("Y", 0, 0, 0))
    own(0, 0)
    got = {0: 0, 1: 0}
    while heap:
        t, _, link, tag = heapq.heappop(heap)
        kind, dz, dh, dx = tag
        step = {"+": 1, "-": -1}.get(link[-1], 0)
        order.append(("recv", link, tag))
        if kind == "Y":
            own(t, 1)
            continue
        if link[0] == "x":
            dx -= step
        else:
            dz -= step
        if kind in ("B1", "A3"):
            far = abs(dz) + 1
            if far <= 3 or (far == 4 and (dh == 0) == (step == 1)):
                send(t, link, (kind, dz, dh, dx))
            if kind == "B1":
                for side in ("x+", "x-"):
                    send(t, side, ("B3", dz, dh, 0))
        else:
            if abs(dx) == 1 and (dh == 0) == (step == 1):
                send(t, link, (kind, dz, dh, dx))
            if kind == "A1":
                got[dh] += 1
                if got[dh] == 3:
                    for side in ("z+", "z-"):
                        send(t, side, ("A3", 0, dh, 0))
    return order


ROWS_A = 32
ORDER = plan(ROWS_A)
SENDS = [op for op in ORDER if op[0] == "send"]
SEND_INDEX = {(op[1], op[2]): i for i, op in enumerate(SENDS)}
NSEM = len(SENDS)


def visiting_order():
    table = []
    for z in range(NZ):
        dist = lambda b: min((b - z) % NZ, (z - b) % NZ)
        top = sorted((b for b in range(4) if b != z), key=dist)
        rest = sorted((b for b in range(4, NZ) if b != z), key=dist)
        table.append([z] + top + rest)
    return [sum(table[z][k] * NZ**z for z in range(NZ)) for k in range(NZ)]


VISIT = visiting_order()


def split(a):
    hi = a.astype(jnp.bfloat16)
    lo = (a - hi.astype(jnp.float32)).astype(jnp.bfloat16)
    return hi, lo


def dot3(a, b):
    ah, al = split(a)
    bh, bl = split(b)
    d = lambda p, q: jnp.dot(p, q, preferred_element_type=jnp.float32)
    return d(ah, bh) + (d(ah, bl) + d(al, bh))


def gather_solve(f_ref, r_ref, g_ref, x_ref, top, cur, inv, ssem, rsem, xs, xr, lsem):
    src = lax.axis_index("src")
    row = lax.axis_index("row")
    z, h, x = src // (NH * NX), lax.rem(src // NX, NH), lax.rem(src, NX)
    core, y_lo = lax.rem(row, 2), row // 2

    def dev(dz=0, flip=False, dx=0):
        zz = lax.rem(z + dz + NZ, NZ)
        hh = 1 - h if flip else h
        return (zz * (NH * NX) + hh * NX + lax.rem(x + dx + NX, NX), row)

    link_to = {"x+": dev(dx=1), "x-": dev(dx=-1), "z+": dev(dz=1), "z-": dev(dz=-1), "y": dev(flip=True)}
    barrier = pltpu.get_barrier_semaphore()
    friends = list(link_to.values()) + [(src, lax.rem(row + i, 4)) for i in (1, 2, 3)]
    for friend in friends:
        pl.semaphore_signal(barrier, inc=1, device_id=friend, device_id_type=MESH)
    keep = pltpu.make_async_copy(f_ref, g_ref.at[z, h, x], lsem.at[0])
    keep.start()
    fetch = pltpu.make_async_copy(r_ref.at[pl.ds(0, COLS)], cur, lsem.at[1])
    solver = jnp.logical_and(core == 0, y_lo == 0)

    @pl.when(solver)
    def _():
        fetch.start()

    pl.semaphore_wait(barrier, len(friends))

    def remote(a, b, s, r, to):
        return pltpu.make_async_remote_copy(
            src_ref=a, dst_ref=b, send_sem=s, recv_sem=r, device_id=to, device_id_type=MESH
        )

    def xblock(ref, j):
        return ref.at[pl.ds(j * BLK, BLK)]

    def x_send(j, k, local=True):
        to = (src, k)
        i = j + STEPS * (0 if k == 2 or k == 3 else 1)
        return remote(xblock(cur if local else x_ref, j), xblock(x_ref, j), xs.at[i], xr.at[j], to)

    SY, SOWN, SZ, SX = 0, 1, 5, 21
    RY, RZ, RX = 0, 1, 17

    @pl.when(core == 0)
    def _():
        piece = lambda zz, dh, xx: g_ref.at[zz, h if dh == 0 else 1 - h, xx]
        zs = [lax.rem(lax.shift_right_logical(jnp.int32(VISIT[k]), 3 * z), NZ) for k in range(NZ)]
        me = f_ref
        xl, xr_ = lax.rem(x + 3, NX), lax.rem(x + 1, NX)
        x2 = lax.rem(x + 2, NX)

        def y_copy():
            return remote(me, piece(z, 0, x), ssem.at[SY], rsem.at[RY], link_to["y"])

        def own_z(dh, side):
            a = me if dh == 0 else piece(z, 1, x)
            return remote(a, piece(z, dh, x), ssem.at[SOWN + 2 * dh + (side == "z-")], rsem.at[RZ + z * 2 + dh], link_to[side])

        def z_copy(k, dh):
            b = zs[k]
            d = lax.rem(z - b + NZ, NZ)
            tz = lax.rem(z + 1 - 2 * (d // 4) + NZ, NZ)
            go = jnp.logical_or(d <= 3 - dh, d >= 6 - dh)
            i = b * 2 + dh
            return go, remote(
                piece(b, dh, x), piece(b, dh, x), ssem.at[SZ + i], rsem.at[RZ + i],
                (tz * (NH * NX) + h * NX + x, row),
            )

        def x_copy(k, dh, which):
            b = zs[k]
            i = (b * 2 + dh) * 3 + which
            if which == 2:
                at = xl if dh == 0 else xr_
                to = link_to["x+"] if dh == 0 else link_to["x-"]
                a = piece(b, dh, at)
                return remote(a, a, ssem.at[SX + i], rsem.at[RX + i], to)
            a = me if k == 0 and dh == 0 else piece(b, dh, x)
            return remote(a, piece(b, dh, x), ssem.at[SX + i], rsem.at[RX + i], link_to["x+" if which == 0 else "x-"])

        def x_arrive(k, dh, which):
            b = zs[k]
            i = (b * 2 + dh) * 3 + which
            at = (xl, xr_, x2)[which]
            a = piece(b, dh, at)
            remote(a, a, ssem.at[SX + i], rsem.at[RX + i], link_to["x+"]).wait_recv()

        def z_part(k):
            for dh in (0, 1):
                go, c = z_copy(k, dh)
                c.wait_recv()
                pl.when(go)(c.start)

        def x_part(k):
            for dh in (0, 1):
                x_copy(k, dh, 0).start()
                x_copy(k, dh, 1).start()

        def x_on(k):
            x_arrive(k, 0, 0)
            x_copy(k, 0, 2).start()
            x_arrive(k, 1, 1)
            x_copy(k, 1, 2).start()

        def x_rest(k):
            x_arrive(k, 0, 1)
            x_arrive(k, 1, 0)
            x_arrive(k, 0, 2)
            x_arrive(k, 1, 2)

        y_copy().start()
        for side in ("z+", "z-"):
            own_z(0, side).start()
        x_copy(0, 0, 0).start()
        x_copy(0, 0, 1).start()
        remote(piece(z, 1, x), piece(z, 1, x), ssem.at[SY], rsem.at[RY], link_to["y"]).wait_recv()
        for side in ("z+", "z-"):
            own_z(1, side).start()
        x_copy(0, 1, 0).start()
        x_copy(0, 1, 1).start()
        for k in (1, 2, 3, 4):
            z_part(k)
            x_part(k)
            x_on(k - 1)
            if k >= 3:
                z_part(k + 2)
        x_on(4)
        z_part(7)
        for k in (5, 6, 7):
            x_part(k)
        for k in range(5):
            x_rest(k)

        @pl.when(y_lo == 0)
        def _():
            keep.wait()
            rows = NH * NX * PIECE
            loads = []
            for b in range(4):
                n = min(rows, COLS - b * rows)
                for q in range(0, n, PIECE):
                    hh, xx = q // (NX * PIECE), (q // PIECE) % NX
                    m = min(PIECE, n - q)
                    loads.append(pltpu.make_async_copy(
                        g_ref.at[b, hh, xx, pl.ds(0, m)], top.at[pl.ds(b * rows + q, m)], lsem.at[2 + len(loads)]))
            for c in loads:
                c.start()
            for c in loads:
                c.wait()
            fetch.wait()
            ii = lax.broadcasted_iota(jnp.int32, (BLK, BLK), 0)
            jj = lax.broadcasted_iota(jnp.int32, (BLK, BLK), 1)
            for j in range(STEPS):
                a = top[pl.ds(j * BLK, BLK), pl.ds(j * BLK, BLK)]
                dg = jnp.where(ii == jj, a, 0.0)
                dc = 1.0 / jnp.sum(dg, axis=1, keepdims=True)
                dr = 1.0 / jnp.sum(dg, axis=0, keepdims=True)
                pair = jnp.logical_and(ii == jj + 1, lax.rem(ii, 2) == 1)
                inv[j] = jnp.where(ii == jj, dc, jnp.where(pair, -(dc * a) * dr, 0.0))

            def level(t, carry):
                bi, bj = lax.shift_right_logical(ii, t), lax.shift_right_logical(jj, t)
                below = jnp.logical_and(bi == bj + 1, lax.rem(bi, 2) == 1)
                for j in range(STEPS):
                    a = top[pl.ds(j * BLK, BLK), pl.ds(j * BLK, BLK)]
                    v = inv[j]
                    inv[j] = v - dot3(v, dot3(jnp.where(below, a, 0.0), v))
                return carry

            lax.fori_loop(1, 7, level, 0)
            x_on(5)
            for j in range(STEPS):
                solved = dot3(inv[j], cur[pl.ds(j * BLK, BLK)])
                cur[pl.ds(j * BLK, BLK)] = solved
                left = COLS - (j + 1) * BLK
                if left:
                    below = pl.ds((j + 1) * BLK, left)
                    cur[below] = cur[below] - dot3(top[below, pl.ds(j * BLK, BLK)], solved)
                if j >= 1:
                    x_send(j - 1, 2).start()
                    x_send(j - 1, 1).start()
                if j == 1:
                    x_on(6)
                if j == 3:
                    x_on(7)
            store = pltpu.make_async_copy(cur, x_ref, lsem.at[2])
            store.start()
            x_send(STEPS - 1, 2).start()
            x_send(STEPS - 1, 1).start()
            store.wait()
            for j in range(STEPS):
                x_send(j, 2).wait_send()
                x_send(j, 1).wait_send()

        @pl.when(y_lo == 1)
        def _():
            keep.wait()
            x_on(5)
            for j in range(STEPS):
                x_send(j, 3, local=False).wait_recv()
                x_send(j, 3, local=False).start()
                if j == 1:
                    x_on(6)
                if j == 3:
                    x_on(7)
            for j in range(STEPS):
                x_send(j, 3, local=False).wait_send()

        for k in (5, 6, 7):
            x_rest(k)
        y_copy().wait_send()
        for dh in (0, 1):
            for side in ("z+", "z-"):
                own_z(dh, side).wait_send()
            for k in range(NZ):
                if k:
                    go, c = z_copy(k, dh)
                    pl.when(go)(c.wait_send)
                for which in range(3):
                    x_copy(k, dh, which).wait_send()

    @pl.when(core == 1)
    def _():
        def at(tag, own):
            kind, dz, dh, dx = tag
            first, n = {"Y": (0, PIECE), "B1": (ROWS_A, PIECE - ROWS_A), "B3": (ROWS_A, PIECE - ROWS_A),
                        "A1": (0, ROWS_A), "A3": (0, ROWS_A)}[kind]
            rows = pl.ds(first, n)
            zz, hh = lax.rem(z + dz + NZ, NZ), h if dh == 0 else 1 - h
            if kind == "A3":
                g = g_ref.at[zz, hh, :, rows]
            else:
                g = g_ref.at[zz, hh, lax.rem(x + dx + NX, NX), rows]
            if own and dz == 0 and dh == 0 and dx == 0 and kind != "A3":
                return f_ref.at[rows], g
            return g, g

        def sent(link, tag):
            a, b = at(tag, True)
            i = SEND_INDEX[(link, tag)]
            return remote(a, b, ssem.at[i], rsem.at[i], link_to[link])

        def arriving(link, tag):
            kind, dz, dh, dx = tag
            step = {"+": 1, "-": -1}.get(link[-1], 0)
            if link[0] == "z":
                dz -= step
            elif link[0] == "x":
                dx -= step
            else:
                dh = 1 - dh
            _, b = at((kind, dz, dh, dx), False)
            i = SEND_INDEX[(link, tag)]
            return remote(b, b, ssem.at[i], rsem.at[i], link_to[link])

        kept = False
        for op, link, tag in ORDER:
            if op == "send":
                if tag[0] == "A3" and not kept:
                    keep.wait()
                    kept = True
                sent(link, tag).start()
            else:
                arriving(link, tag).wait_recv()
        for _, link, tag in SENDS:
            sent(link, tag).wait_send()
        for j in range(STEPS):
            x_send(j, 3, local=False).wait_recv()


TILE = 512


def update(f_ref, x_ref, r_ref, o_ref, xh, xl):
    i = pl.program_id(0)
    row = lax.axis_index("row")

    @pl.when(i == 0)
    def _():
        hi, lo = split(x_ref[...])
        xh[...] = hi
        xl[...] = lo

    solved = jnp.logical_and(row == 0, i < COLS // TILE)

    @pl.when(solved)
    def _():
        o_ref[...] = x_ref[pl.ds(pl.multiple_of(lax.rem(i, COLS // TILE) * TILE, TILE), TILE)]

    @pl.when(jnp.logical_not(solved))
    def _():
        fh, fl = split(f_ref[...])
        d = lambda p, q: jnp.dot(p, q[...], preferred_element_type=jnp.float32)
        o_ref[...] = r_ref[...] - (d(fh, xh) + (d(fh, xl) + d(fl, xh)))


def local(factor, right_side):
    rows, width = right_side.shape
    ANY = pl.BlockSpec(memory_space=pl.ANY)
    gathered, solved = pl.pallas_call(
        gather_solve,
        out_shape=(
            jax.ShapeDtypeStruct((NZ, NH, NX, PIECE, COLS), jnp.float32),
            jax.ShapeDtypeStruct((COLS, width), jnp.float32),
        ),
        in_specs=[pl.BlockSpec(memory_space=pltpu.VMEM), ANY],
        out_specs=(ANY, ANY),
        scratch_shapes=[
            pltpu.VMEM((COLS, COLS), jnp.float32),
            pltpu.VMEM((COLS, width), jnp.float32),
            pltpu.VMEM((STEPS, BLK, BLK), jnp.float32),
            pltpu.SemaphoreType.DMA((NSEM,)),
            pltpu.SemaphoreType.DMA((NSEM,)),
            pltpu.SemaphoreType.DMA((2 * STEPS,)),
            pltpu.SemaphoreType.DMA((STEPS,)),
            pltpu.SemaphoreType.DMA((32,)),
        ],
        compiler_params=pltpu.CompilerParams(collective_id=0, has_side_effects=True),
    )(factor, right_side)
    return pl.pallas_call(
        update,
        grid=(rows // TILE,),
        out_shape=jax.ShapeDtypeStruct((rows, width), jnp.float32),
        in_specs=[
            pl.BlockSpec((TILE, COLS), lambda i: (i, 0)),
            pl.BlockSpec((COLS, width), lambda i: (0, 0)),
            pl.BlockSpec((TILE, width), lambda i: (i, 0)),
        ],
        out_specs=pl.BlockSpec((TILE, width), lambda i: (i, 0)),
        scratch_shapes=[pltpu.VMEM((COLS, width), jnp.bfloat16), pltpu.VMEM((COLS, width), jnp.bfloat16)],
    )(gathered.reshape(rows, COLS), solved, right_side)


def solution(mesh):
    placed = (P(("row", "src"), None), P("row", "src"))
    return jax.shard_map(
        local, mesh=mesh, in_specs=placed, out_specs=P("row", "src"), check_vma=False
    )
```

time: 365 us -> 129 us (0.35)
  the two profiles are of different devices: /device:TPU:1 before, /device:TPU:89 now
where the time goes in v2:
time: 129 us
  Pallas kernels  129 us (100%)
    pallas_call x1, Pallas kernels, local(): pl.pallas_call(gather_solve, out_shape=(jax.ShapeDtypeStruct((NZ, NH, NX,...  115 us
    pallas_call x1, Pallas kernels, local(): pl.pallas_call(update, grid=(rows // TILE,), out_shape=jax.ShapeDtypeStru...  13.7 us

profile of v2, /device:TPU:89, one launch (start us, length us, event | category | flops | bytes accessed | tf_op | source)
XLA Modules:
  0.0 128.6 jit_solution(2171233653743080999)
XLA Ops:
  0.0 114.8 %shard_map.28 = (f32[8,2,4,40,1024]{4,3,2,1,0:T(8,128)}, f32[1024,512]{1,0:T(8,128)}) custom-call(f32[40,1024]{1,0:T(8,128)} %f_ref.1, f32[2560,512]{1,0:T(8,128)} %r_ref.3), custom_call_target="tpu_custom_call" | custom-call | tf_op jit(solution)/shard_map/pallas_call | solution.py:404
  114.9 13.7 %shard_map.29 = f32[2560,512]{1,0:T(8,128)} custom-call(f32[2560,1024]{1,0:T(8,128)} %bitcast.1, f32[1024,512]{1,0:T(8,128)} %get-tuple-element.8.x_ref, f32[2560,512]{1,0:T(8,128)} %r_ref.3), custom_call_target="tpu_custom_call" | custom-call | tf_op jit(solution)/shard_map/pallas_call | solution.py:424

commit v3 on v0

v3 whole, which is shorter than its diff:
```python
import heapq

import jax
import jax.numpy as jnp
from jax import lax
from jax.experimental import pallas as pl
from jax.experimental.pallas import tpu as pltpu
from jax.sharding import PartitionSpec as P

MESH = pl.DeviceIdType.MESH
NX, NH, NZ = 4, 2, 8
PIECE = 40
COLS = 1024
WIDTH = 512
BLK = 128
STEPS = COLS // BLK
PIECES = -(-COLS // PIECE)
BANDS = -(-PIECES // NX)
UNITS = PIECES + BANDS
TOPZ = -(-PIECES // (NX * NH))
CHUNKS = 4
RATE = {"x+": 46e3, "x-": 46e3, "z+": 46e3, "z-": 46e3, "y": 23e3}


def plan(rows_a, latency=1.7):
    size = {"Y": PIECE, "B1": PIECE - rows_a, "B3": PIECE - rows_a, "A1": rows_a, "A3": 4 * rows_a}
    free = dict.fromkeys(RATE, 0.0)
    heap, order = [], []

    def send(t, link, tag):
        end = max(t, free[link]) + size[tag[0]] * 4096 / RATE[link]
        free[link] = end
        heapq.heappush(heap, (end + latency, len(order), link, tag))
        order.append(("send", link, tag))

    def own(t, dh):
        for link in ("z+", "z-"):
            send(t, link, ("B1", 0, dh, 0))
        for link in ("x+", "x-"):
            send(t, link, ("A1", 0, dh, 0))
        for link in ("x+", "x-"):
            send(t, link, ("B3", 0, dh, 0))

    send(0, "y", ("Y", 0, 0, 0))
    own(0, 0)
    got = {0: 0, 1: 0}
    while heap:
        t, _, link, tag = heapq.heappop(heap)
        kind, dz, dh, dx = tag
        step = {"+": 1, "-": -1}.get(link[-1], 0)
        order.append(("recv", link, tag))
        if kind == "Y":
            own(t, 1)
            continue
        if link[0] == "x":
            dx -= step
        else:
            dz -= step
        if kind in ("B1", "A3"):
            far = abs(dz) + 1
            if far <= 3 or (far == 4 and (dh == 0) == (step == 1)):
                send(t, link, (kind, dz, dh, dx))
            if kind == "B1":
                for side in ("x+", "x-"):
                    send(t, side, ("B3", dz, dh, 0))
        else:
            if abs(dx) == 1 and (dh == 0) == (step == 1):
                send(t, link, (kind, dz, dh, dx))
            if kind == "A1":
                got[dh] += 1
                if got[dh] == 3:
                    for side in ("z+", "z-"):
                        send(t, side, ("A3", 0, dh, 0))
    return order


ROWS_A = 16
ORDER = plan(ROWS_A)
SENDS = [op for op in ORDER if op[0] == "send"]
SEND_INDEX = {(op[1], op[2]): i for i, op in enumerate(SENDS)}
NSEM = len(SENDS)


def split(a):
    hi = a.astype(jnp.bfloat16)
    lo = (a - hi.astype(jnp.float32)).astype(jnp.bfloat16)
    return hi, lo


def dot3(a, b):
    ah, al = split(a)
    bh, bl = split(b)
    d = lambda p, q: jnp.dot(p, q, preferred_element_type=jnp.float32)
    return d(ah, bh) + (d(ah, bl) + d(al, bh))


def gather_solve(f_ref, r_ref, g_ref, x_ref, t_ref, top, cur, inv, ssem, rsem, xs, xr, ts, tr, lsem):
    src = lax.axis_index("src")
    row = lax.axis_index("row")
    z, h, x = src // (NH * NX), lax.rem(src // NX, NH), lax.rem(src, NX)
    core, y_lo = lax.rem(row, 2), row // 2

    def dev(dz=0, flip=False, dx=0):
        zz = lax.rem(z + dz + NZ, NZ)
        hh = 1 - h if flip else h
        return (zz * (NH * NX) + hh * NX + lax.rem(x + dx + NX, NX), row)

    link_to = {"x+": dev(dx=1), "x-": dev(dx=-1), "z+": dev(dz=1), "z-": dev(dz=-1), "y": dev(flip=True)}
    beside = (src, row + 1 - 2 * core)
    across = ((src, lax.rem(row + 2, 4)), (dev(flip=True)[0], lax.rem(row + 2, 4)))
    barrier = pltpu.get_barrier_semaphore()
    friends = list(link_to.values()) + [beside, *across]
    for friend in friends:
        pl.semaphore_signal(barrier, inc=1, device_id=friend, device_id_type=MESH)
    keep = pltpu.make_async_copy(f_ref, g_ref.at[z, h, x], lsem.at[0])
    keep.start()
    fetch = pltpu.make_async_copy(r_ref.at[pl.ds(0, COLS)], cur, lsem.at[1])
    first = jnp.logical_and(core == 0, y_lo == 0)
    pl.when(first)(fetch.start)
    pl.semaphore_wait(barrier, len(friends))

    def remote(a, b, s, r, to):
        return pltpu.make_async_remote_copy(
            src_ref=a, dst_ref=b, send_sem=s, recv_sem=r, device_id=to, device_id_type=MESH
        )

    ROWS = {"Y": (0, PIECE), "B1": (ROWS_A, PIECE - ROWS_A), "B3": (ROWS_A, PIECE - ROWS_A),
            "A1": (0, ROWS_A), "A3": (0, ROWS_A)}

    def where(tag):
        kind, dz, dh, dx = tag
        rows = pl.ds(*ROWS[kind])
        zz, hh = lax.rem(z + dz + NZ, NZ), h if dh == 0 else 1 - h
        return (zz, hh, slice(None), rows) if kind == "A3" else (zz, hh, lax.rem(x + dx + NX, NX), rows)

    def sent(i):
        _, link, tag = SENDS[i]
        b = g_ref.at[where(tag)]
        a = f_ref.at[pl.ds(*ROWS[tag[0]])] if tag[1:] == (0, 0, 0) and tag[0] != "A3" else b
        return remote(a, b, ssem.at[i], rsem.at[i], link_to[link])

    def landed(i):
        _, link, (kind, dz, dh, dx) = SENDS[i]
        step = {"+": 1, "-": -1}.get(link[-1], 0)
        if link[0] == "z":
            dz -= step
        elif link[0] == "x":
            dx -= step
        else:
            dh = 1 - dh
        return kind, dz, dh, dx

    handed = []

    def up(tag, half):
        kind, dz, dh, dx = tag
        zz, hh, xx, rows = where(tag)
        if kind == "A3":
            unit, count = zz * NH + hh, BANDS
            base = PIECES
        else:
            unit, count = (zz * NH + hh) * NX + xx, PIECES
            base = 0
        go = jnp.logical_and(first, unit < count)
        if half == 0:
            go = jnp.logical_and(go, zz >= 1)
        elif dh == 1:
            go = jnp.logical_and(go, zz == 0)
        i = base + lax.min(unit, count - 1)
        at = (lax.min(zz, TOPZ - 1), hh, xx, rows)
        a = f_ref.at[rows] if tag[1:] == (0, 0, 0) and kind != "A3" else g_ref.at[where(tag)]
        return go, remote(a, t_ref.at[at], ts.at[half * UNITS + i], tr.at[i], across[half])

    def hand_up(tag):
        for half in (0, 1) if tag[2] == 0 else (1,):
            go, c = up(tag, half)
            pl.when(go)(c.start)
            handed.append((tag, half))

    def right(i):
        rows = pl.ds(i * (COLS // CHUNKS), COLS // CHUNKS)
        return remote(r_ref.at[rows], cur.at[rows], ts.at[2 * UNITS + i], tr.at[UNITS + i], across[0])

    kept = False
    arrived = 0
    for op, link, tag in ORDER:
        i = SEND_INDEX[(link, tag)]
        if op == "send":
            if tag[0] == "A3" and not kept:
                keep.wait()
                kept = True
            sent(i).start()
            if link == "z+" and tag[1] == 0:
                hand_up(("A3", 0, tag[2], 0) if tag[0] == "A3" else ("B3", 0, tag[2], 0))
            continue
        got = landed(i)
        b = g_ref.at[where(got)]
        remote(b, b, ssem.at[i], rsem.at[i], link_to[link]).wait_recv()
        if got[0] in ("A3", "B3"):
            hand_up(got)
        elif got[0] == "B1":
            hand_up(("B3",) + got[1:])
        arrived += 1
        if arrived % 12 == 11 and arrived // 12 < CHUNKS:
            pl.when(first)(right(arrived // 12).start)

    def x_send(j):
        rows = pl.ds(j * BLK, BLK)
        return remote(cur.at[rows], x_ref.at[rows], xs.at[j], xr.at[j], beside)

    @pl.when(core == 0)
    def _():
        def load(ref):
            loads = []
            for p in range(PIECES):
                loads.append(pltpu.make_async_copy(
                    ref.at[p // (NH * NX), p // NX % NH, p % NX], top.at[pl.ds(p * PIECE, PIECE)], lsem.at[2 + p]))
            for c in loads:
                c.start()
            for c in loads:
                c.wait()

        @pl.when(y_lo == 0)
        def _():
            load(g_ref)
            fetch.wait()

        @pl.when(y_lo == 1)
        def _():
            for p in range(PIECES):
                a = t_ref.at[p // (NH * NX), p // NX % NH, p % NX, pl.ds(ROWS_A, PIECE - ROWS_A)]
                remote(a, a, ts.at[p], tr.at[p], across[0]).wait_recv()
            for u in range(BANDS):
                a = t_ref.at[u // NH, u % NH, :, pl.ds(0, ROWS_A)]
                remote(a, a, ts.at[PIECES + u], tr.at[PIECES + u], across[0]).wait_recv()
            load(t_ref)
            for i in range(CHUNKS):
                right(i).wait_recv()

        ii = lax.broadcasted_iota(jnp.int32, (BLK, BLK), 0)
        jj = lax.broadcasted_iota(jnp.int32, (BLK, BLK), 1)
        for j in range(STEPS):
            a = top[pl.ds(j * BLK, BLK), pl.ds(j * BLK, BLK)]
            dg = jnp.where(ii == jj, a, 0.0)
            dc = 1.0 / jnp.sum(dg, axis=1, keepdims=True)
            dr = 1.0 / jnp.sum(dg, axis=0, keepdims=True)
            pair = jnp.logical_and(ii == jj + 1, lax.rem(ii, 2) == 1)
            inv[j] = jnp.where(ii == jj, dc, jnp.where(pair, -(dc * a) * dr, 0.0))

        def level(t, carry):
            bi, bj = lax.shift_right_logical(ii, t), lax.shift_right_logical(jj, t)
            below = jnp.logical_and(bi == bj + 1, lax.rem(bi, 2) == 1)
            for j in range(STEPS):
                a = top[pl.ds(j * BLK, BLK), pl.ds(j * BLK, BLK)]
                v = inv[j]
                inv[j] = v - dot3(v, dot3(jnp.where(below, a, 0.0), v))
            return carry

        lax.fori_loop(1, 7, level, 0)
        for j in range(STEPS):
            rows = pl.ds(j * BLK, BLK)
            solved = dot3(inv[j], cur[rows])
            cur[rows] = solved
            left = COLS - (j + 1) * BLK
            if left:
                below = pl.ds((j + 1) * BLK, left)
                cur[below] = cur[below] - dot3(top[below, rows], solved)
            if j >= 1:
                x_send(j - 1).start()
        store = pltpu.make_async_copy(cur, x_ref, lsem.at[2])
        store.start()
        x_send(STEPS - 1).start()
        store.wait()
        for j in range(STEPS):
            x_send(j).wait_send()

    @pl.when(core == 1)
    def _():
        for j in range(STEPS):
            x_send(j).wait_recv()

    for i in range(NSEM):
        sent(i).wait_send()
    for tag, half in handed:
        go, c = up(tag, half)
        pl.when(go)(c.wait_send)

    @pl.when(first)
    def _():
        for i in range(CHUNKS):
            right(i).wait_send()


TILE = 512


def update(f_ref, x_ref, r_ref, o_ref, xh, xl):
    i = pl.program_id(0)
    row = lax.axis_index("row")

    @pl.when(i == 0)
    def _():
        hi, lo = split(x_ref[...])
        xh[...] = hi
        xl[...] = lo

    solved = jnp.logical_and(row == 0, i < COLS // TILE)

    @pl.when(solved)
    def _():
        o_ref[...] = x_ref[pl.ds(pl.multiple_of(lax.rem(i, COLS // TILE) * TILE, TILE), TILE)]

    @pl.when(jnp.logical_not(solved))
    def _():
        fh, fl = split(f_ref[...])
        d = lambda p, q: jnp.dot(p, q[...], preferred_element_type=jnp.float32)
        o_ref[...] = r_ref[...] - (d(fh, xh) + (d(fh, xl) + d(fl, xh)))


def local(factor, right_side):
    rows, width = right_side.shape
    ANY = pl.BlockSpec(memory_space=pl.ANY)
    gathered, solved, _ = pl.pallas_call(
        gather_solve,
        out_shape=(
            jax.ShapeDtypeStruct((NZ, NH, NX, PIECE, COLS), jnp.float32),
            jax.ShapeDtypeStruct((COLS, width), jnp.float32),
            jax.ShapeDtypeStruct((TOPZ, NH, NX, PIECE, COLS), jnp.float32),
        ),
        in_specs=[pl.BlockSpec(memory_space=pltpu.VMEM), ANY],
        out_specs=(ANY, ANY, ANY),
        scratch_shapes=[
            pltpu.VMEM((PIECES * PIECE, COLS), jnp.float32),
            pltpu.VMEM((COLS, width), jnp.float32),
            pltpu.VMEM((STEPS, BLK, BLK), jnp.float32),
            pltpu.SemaphoreType.DMA((NSEM,)),
            pltpu.SemaphoreType.DMA((NSEM,)),
            pltpu.SemaphoreType.DMA((STEPS,)),
            pltpu.SemaphoreType.DMA((STEPS,)),
            pltpu.SemaphoreType.DMA((2 * UNITS + CHUNKS,)),
            pltpu.SemaphoreType.DMA((UNITS + CHUNKS,)),
            pltpu.SemaphoreType.DMA((32,)),
        ],
        compiler_params=pltpu.CompilerParams(collective_id=0, has_side_effects=True),
    )(factor, right_side)
    return pl.pallas_call(
        update,
        grid=(rows // TILE,),
        out_shape=jax.ShapeDtypeStruct((rows, width), jnp.float32),
        in_specs=[
            pl.BlockSpec((TILE, COLS), lambda i: (i, 0)),
            pl.BlockSpec((COLS, width), lambda i: (0, 0)),
            pl.BlockSpec((TILE, width), lambda i: (i, 0)),
        ],
        out_specs=pl.BlockSpec((TILE, width), lambda i: (i, 0)),
        scratch_shapes=[pltpu.VMEM((COLS, width), jnp.bfloat16), pltpu.VMEM((COLS, width), jnp.bfloat16)],
    )(gathered.reshape(rows, COLS), solved, right_side)


def solution(mesh):
    placed = (P(("row", "src"), None), P("row", "src"))
    return jax.shard_map(
        local, mesh=mesh, in_specs=placed, out_specs=P("row", "src"), check_vma=False
    )
```

time: 365 us -> 104 us (0.28)
  the two profiles are of different devices: /device:TPU:1 before, /device:TPU:137 now
where the time goes in v3:
time: 104 us
  Pallas kernels  104 us (100%)
    pallas_call x1, Pallas kernels, local(): pl.pallas_call(gather_solve, out_shape=(jax.ShapeDtypeStruct((NZ, NH, NX,...  90.5 us
    pallas_call x1, Pallas kernels, local(): pl.pallas_call(update, grid=(rows // TILE,), out_shape=jax.ShapeDtypeStru...  13.7 us

profile of v3, /device:TPU:137, one launch (start us, length us, event | category | flops | bytes accessed | tf_op | source)
XLA Modules:
  0.0 104.2 jit_solution(8965969088892756468)
XLA Ops:
  0.0 90.5 %shard_map.28 = (f32[8,2,4,40,1024]{4,3,2,1,0:T(8,128)}, f32[1024,512]{1,0:T(8,128)}, f32[4,2,4,40,1024]{4,3,2,1,0:T(8,128)}) custom-call(f32[40,1024]{1,0:T(8,128)} %f_ref.1, f32[2560,512]{1,0:T(8,128)} %r_ref.3), custom_call_target="tpu_custom_call" | custom-call | tf_op jit(solution)/shard_map/pallas_call | solution.py:323
  90.5 13.7 %shard_map.29 = f32[2560,512]{1,0:T(8,128)} custom-call(f32[2560,1024]{1,0:T(8,128)} %bitcast.1, f32[1024,512]{1,0:T(8,128)} %get-tuple-element.8.x_ref, f32[2560,512]{1,0:T(8,128)} %r_ref.3), custom_call_target="tpu_custom_call" | custom-call | tf_op jit(solution)/shard_map/pallas_call | solution.py:346

commit v4 on v3

--- a/solution.py
+++ b/solution.py
@@ -15,10 +15,9 @@
 BLK = 128
 STEPS = COLS // BLK
 PIECES = -(-COLS // PIECE)
-BANDS = -(-PIECES // NX)
-UNITS = PIECES + BANDS
-TOPZ = -(-PIECES // (NX * NH))
+UNITS = 2 * PIECES
 CHUNKS = 4
+GATE = 32
 RATE = {"x+": 46e3, "x-": 46e3, "z+": 46e3, "z-": 46e3, "y": 23e3}
 
 
@@ -87,14 +86,17 @@
     return hi, lo
 
 
-def dot3(a, b):
-    ah, al = split(a)
-    bh, bl = split(b)
+def dot3s(a, b):
+    (ah, al), (bh, bl) = a, b
     d = lambda p, q: jnp.dot(p, q, preferred_element_type=jnp.float32)
     return d(ah, bh) + (d(ah, bl) + d(al, bh))
 
 
-def gather_solve(f_ref, r_ref, g_ref, x_ref, t_ref, top, cur, inv, ssem, rsem, xs, xr, ts, tr, lsem):
+def dot3(a, b):
+    return dot3s(split(a), split(b))
+
+
+def gather_solve(f_ref, r_ref, g_ref, x_ref, top, cur, inv, ssem, rsem, xs, xr, ts, tr, tl, lsem, gate):
     src = lax.axis_index("src")
     row = lax.axis_index("row")
     z, h, x = src // (NH * NX), lax.rem(src // NX, NH), lax.rem(src, NX)
@@ -152,34 +154,39 @@
 
     handed = []
 
-    def up(tag, half):
+    def units(tag):
         kind, dz, dh, dx = tag
-        zz, hh, xx, rows = where(tag)
-        if kind == "A3":
-            unit, count = zz * NH + hh, BANDS
-            base = PIECES
-        else:
-            unit, count = (zz * NH + hh) * NX + xx, PIECES
-            base = 0
-        go = jnp.logical_and(first, unit < count)
-        if half == 0:
-            go = jnp.logical_and(go, zz >= 1)
-        elif dh == 1:
-            go = jnp.logical_and(go, zz == 0)
-        i = base + lax.min(unit, count - 1)
-        at = (lax.min(zz, TOPZ - 1), hh, xx, rows)
-        a = f_ref.at[rows] if tag[1:] == (0, 0, 0) and kind != "A3" else g_ref.at[where(tag)]
-        return go, remote(a, t_ref.at[at], ts.at[half * UNITS + i], tr.at[i], across[half])
+        start, n = ROWS[kind]
+        zz, hh = lax.rem(z + dz + NZ, NZ), h if dh == 0 else 1 - h
+        for e in range(NX) if kind == "A3" else (dx,):
+            xx = e if kind == "A3" else lax.rem(x + dx + NX, NX)
+            p = (zz * NH + hh) * NX + xx
+            own = kind == "B3" and tag[1:] == (0, 0, 0)
+            a = f_ref.at[pl.ds(start, n)] if own else g_ref.at[zz, hh, xx, pl.ds(start, n)]
+            yield zz, lax.min(p, PIECES - 1), jnp.logical_and(first, p < PIECES), a, (0 if kind == "A3" else PIECES), (start, n)
+
+    def copies(tag):
+        for zz, p, go, a, base, (start, n) in units(tag):
+            b = top.at[pl.ds(p * PIECE + start, n)]
+            yield go, pltpu.make_async_copy(a, b, tl.at[base + p]), False
+            if tag[2] == 0:
+                yield jnp.logical_and(go, zz >= 1), remote(a, b, ts.at[base + p], tr.at[base + p], across[0]), True
+                yield go, remote(a, b, ts.at[UNITS + base + p], tr.at[base + p], across[1]), True
+            else:
+                yield jnp.logical_and(go, zz == 0), remote(a, b, ts.at[UNITS + base + p], tr.at[base + p], across[1]), True
 
     def hand_up(tag):
-        for half in (0, 1) if tag[2] == 0 else (1,):
-            go, c = up(tag, half)
+        for go, c, _ in copies(tag):
             pl.when(go)(c.start)
-            handed.append((tag, half))
+        handed.append(tag)
 
     def right(i):
         rows = pl.ds(i * (COLS // CHUNKS), COLS // CHUNKS)
         return remote(r_ref.at[rows], cur.at[rows], ts.at[2 * UNITS + i], tr.at[UNITS + i], across[0])
+
+    @pl.when(core == 1)
+    def _():
+        pl.semaphore_wait(gate, 1)
 
     kept = False
     arrived = 0
@@ -191,7 +198,11 @@
                 kept = True
             sent(i).start()
             if link == "z+" and tag[1] == 0:
-                hand_up(("A3", 0, tag[2], 0) if tag[0] == "A3" else ("B3", 0, tag[2], 0))
+                if tag[0] == "A3":
+                    hand_up(("A3", 0, tag[2], 0))
+                elif tag[2] == 1:
+                    hand_up(("B3", 0, 0, 0))
+                    hand_up(("B3", 0, 1, 0))
             continue
         got = landed(i)
         b = g_ref.at[where(got)]
@@ -201,6 +212,11 @@
         elif got[0] == "B1":
             hand_up(("B3",) + got[1:])
         arrived += 1
+        if arrived == GATE:
+            @pl.when(core == 0)
+            def _():
+                pl.semaphore_signal(gate, inc=1, device_id=beside, device_id_type=MESH)
+
         if arrived % 12 == 11 and arrived // 12 < CHUNKS:
             pl.when(first)(right(arrived // 12).start)
 
@@ -210,30 +226,22 @@
 
     @pl.when(core == 0)
     def _():
-        def load(ref):
-            loads = []
-            for p in range(PIECES):
-                loads.append(pltpu.make_async_copy(
-                    ref.at[p // (NH * NX), p // NX % NH, p % NX], top.at[pl.ds(p * PIECE, PIECE)], lsem.at[2 + p]))
-            for c in loads:
-                c.start()
-            for c in loads:
-                c.wait()
+        def part(p, base):
+            start, n = ROWS["A3"] if base == 0 else ROWS["B3"]
+            return top.at[pl.ds(p * PIECE + start, n)]
 
         @pl.when(y_lo == 0)
         def _():
-            load(g_ref)
+            for base in (0, PIECES):
+                for p in range(PIECES):
+                    pltpu.make_async_copy(part(p, base), part(p, base), tl.at[base + p]).wait()
             fetch.wait()
 
         @pl.when(y_lo == 1)
         def _():
-            for p in range(PIECES):
-                a = t_ref.at[p // (NH * NX), p // NX % NH, p % NX, pl.ds(ROWS_A, PIECE - ROWS_A)]
-                remote(a, a, ts.at[p], tr.at[p], across[0]).wait_recv()
-            for u in range(BANDS):
-                a = t_ref.at[u // NH, u % NH, :, pl.ds(0, ROWS_A)]
-                remote(a, a, ts.at[PIECES + u], tr.at[PIECES + u], across[0]).wait_recv()
-            load(t_ref)
+            for base in (0, PIECES):
+                for p in range(PIECES):
+                    remote(part(p, base), part(p, base), ts.at[base + p], tr.at[base + p], across[0]).wait_recv()
             for i in range(CHUNKS):
                 right(i).wait_recv()
 
@@ -250,10 +258,12 @@
         def level(t, carry):
             bi, bj = lax.shift_right_logical(ii, t), lax.shift_right_logical(jj, t)
             below = jnp.logical_and(bi == bj + 1, lax.rem(bi, 2) == 1)
+            v = [split(inv[j]) for j in range(STEPS)]
+            e = [split(jnp.where(below, top[pl.ds(j * BLK, BLK), pl.ds(j * BLK, BLK)], 0.0)) for j in range(STEPS)]
+            w = [split(dot3s(e[j], v[j])) for j in range(STEPS)]
+            w = [dot3s(v[j], w[j]) for j in range(STEPS)]
             for j in range(STEPS):
-                a = top[pl.ds(j * BLK, BLK), pl.ds(j * BLK, BLK)]
-                v = inv[j]
-                inv[j] = v - dot3(v, dot3(jnp.where(below, a, 0.0), v))
+                inv[j] = inv[j] - w[j]
             return carry
 
         lax.fori_loop(1, 7, level, 0)
@@ -281,9 +291,10 @@
 
     for i in range(NSEM):
         sent(i).wait_send()
-    for tag, half in handed:
-        go, c = up(tag, half)
-        pl.when(go)(c.wait_send)
+    for tag in handed:
+        for go, c, away in copies(tag):
+            if away:
+                pl.when(go)(c.wait_send)
 
     @pl.when(first)
     def _():
@@ -294,41 +305,57 @@
 TILE = 512
 
 
-def update(f_ref, x_ref, r_ref, o_ref, xh, xl):
-    i = pl.program_id(0)
+def update(f_ref, x_ref, r_ref, o_ref, fb, rb, ob, xb, xh, xl, sems):
     row = lax.axis_index("row")
-
-    @pl.when(i == 0)
-    def _():
-        hi, lo = split(x_ref[...])
-        xh[...] = hi
-        xl[...] = lo
-
-    solved = jnp.logical_and(row == 0, i < COLS // TILE)
-
-    @pl.when(solved)
-    def _():
-        o_ref[...] = x_ref[pl.ds(pl.multiple_of(lax.rem(i, COLS // TILE) * TILE, TILE), TILE)]
-
-    @pl.when(jnp.logical_not(solved))
-    def _():
-        fh, fl = split(f_ref[...])
+    n = f_ref.shape[0] // TILE
+    tile = lambda i: pl.ds(i * TILE, TILE)
+    get_x = pltpu.make_async_copy(x_ref, xb, sems.at[0])
+    get_f = [pltpu.make_async_copy(f_ref.at[tile(i)], fb.at[tile(i)], sems.at[1 + i]) for i in range(n)]
+    get_r = [pltpu.make_async_copy(r_ref.at[tile(i)], rb.at[tile(i)], sems.at[1 + n + i]) for i in range(n)]
+    put = [pltpu.make_async_copy(ob.at[tile(i)], o_ref.at[tile(i)], sems.at[1 + 2 * n + i]) for i in range(n)]
+    get_x.start()
+    for f, r in zip(get_f, get_r):
+        f.start()
+        r.start()
+    get_x.wait()
+    hi, lo = split(xb[...])
+    xh[...] = hi
+    xl[...] = lo
+
+    def advance(i):
+        fh, fl = split(fb[tile(i)])
         d = lambda p, q: jnp.dot(p, q[...], preferred_element_type=jnp.float32)
-        o_ref[...] = r_ref[...] - (d(fh, xh) + (d(fh, xl) + d(fl, xh)))
+        ob[tile(i)] = rb[tile(i)] - (d(fh, xh) + (d(fh, xl) + d(fl, xh)))
+
+    for i in range(n):
+        get_f[i].wait()
+        get_r[i].wait()
+        if i < COLS // TILE:
+            @pl.when(row == 0)
+            def _():
+                ob[tile(i)] = xb[tile(i)]
+
+            @pl.when(row != 0)
+            def _():
+                advance(i)
+        else:
+            advance(i)
+        put[i].start()
+    for c in put:
+        c.wait()
 
 
 def local(factor, right_side):
     rows, width = right_side.shape
     ANY = pl.BlockSpec(memory_space=pl.ANY)
-    gathered, solved, _ = pl.pallas_call(
+    gathered, solved = pl.pallas_call(
         gather_solve,
         out_shape=(
             jax.ShapeDtypeStruct((NZ, NH, NX, PIECE, COLS), jnp.float32),
             jax.ShapeDtypeStruct((COLS, width), jnp.float32),
-            jax.ShapeDtypeStruct((TOPZ, NH, NX, PIECE, COLS), jnp.float32),
         ),
         in_specs=[pl.BlockSpec(memory_space=pltpu.VMEM), ANY],
-        out_specs=(ANY, ANY, ANY),
+        out_specs=(ANY, ANY),
         scratch_shapes=[
             pltpu.VMEM((PIECES * PIECE, COLS), jnp.float32),
             pltpu.VMEM((COLS, width), jnp.float32),
@@ -339,21 +366,26 @@
             pltpu.SemaphoreType.DMA((STEPS,)),
             pltpu.SemaphoreType.DMA((2 * UNITS + CHUNKS,)),
             pltpu.SemaphoreType.DMA((UNITS + CHUNKS,)),
-            pltpu.SemaphoreType.DMA((32,)),
+            pltpu.SemaphoreType.DMA((UNITS,)),
+            pltpu.SemaphoreType.DMA((3,)),
+            pltpu.SemaphoreType.REGULAR,
         ],
         compiler_params=pltpu.CompilerParams(collective_id=0, has_side_effects=True),
     )(factor, right_side)
     return pl.pallas_call(
         update,
-        grid=(rows // TILE,),
         out_shape=jax.ShapeDtypeStruct((rows, width), jnp.float32),
-        in_specs=[
-            pl.BlockSpec((TILE, COLS), lambda i: (i, 0)),
-            pl.BlockSpec((COLS, width), lambda i: (0, 0)),
-            pl.BlockSpec((TILE, width), lambda i: (i, 0)),
+        in_specs=[ANY, ANY, ANY],
+        out_specs=ANY,
+        scratch_shapes=[
+            pltpu.VMEM((rows, COLS), jnp.float32),
+            pltpu.VMEM((rows, width), jnp.float32),
+            pltpu.VMEM((rows, width), jnp.float32),
+            pltpu.VMEM((COLS, width), jnp.float32),
+            pltpu.VMEM((COLS, width), jnp.bfloat16),
+            pltpu.VMEM((COLS, width), jnp.bfloat16),
+            pltpu.SemaphoreType.DMA((3 * rows // TILE + 1,)),
         ],
-        out_specs=pl.BlockSpec((TILE, width), lambda i: (i, 0)),
-        scratch_shapes=[pltpu.VMEM((COLS, width), jnp.bfloat16), pltpu.VMEM((COLS, width), jnp.bfloat16)],
     )(gathered.reshape(rows, COLS), solved, right_side)
 
 

time: 104 us -> 94.5 us (0.909)
  the two profiles are of different devices: /device:TPU:137 before, /device:TPU:1 now
where the time goes in v4:
time: 94.5 us; the launch traced here: 94.4 us
  Pallas kernels  94.2 us (100%)
    pallas_call x1, Pallas kernels, local(): pl.pallas_call(gather_solve, out_shape=(jax.ShapeDtypeStruct((NZ, NH, NX,...  81.5 us
    pallas_call x1, Pallas kernels, local(): pl.pallas_call(update, out_shape=jax.ShapeDtypeStruct((rows, width), jnp....  12.7 us

profile of v4, /device:TPU:1, one launch (start us, length us, event | category | flops | bytes accessed | tf_op | source)
XLA Modules:
  0.0 94.4 jit_solution(16491059788134734823)
XLA Ops:
  0.0 81.5 %shard_map.28 = (f32[8,2,4,40,1024]{4,3,2,1,0:T(8,128)}, f32[1024,512]{1,0:T(8,128)}) custom-call(f32[40,1024]{1,0:T(8,128)} %f_ref.1, f32[2560,512]{1,0:T(8,128)} %r_ref.3), custom_call_target="tpu_custom_call" | custom-call | tf_op jit(solution)/shard_map/pallas_call | solution.py:351
  81.5 12.7 %shard_map.29 = f32[2560,512]{1,0:T(8,128)} custom-call(f32[2560,1024]{1,0:T(8,128)} %bitcast.1, f32[1024,512]{1,0:T(8,128)} %get-tuple-element.8.x_ref, f32[2560,512]{1,0:T(8,128)} %r_ref.3), custom_call_target="tpu_custom_call" | custom-call | tf_op jit(solution)/shard_map/pallas_call | solution.py:375

commit v5 on v4

--- a/solution.py
+++ b/solution.py
@@ -17,8 +17,8 @@
 PIECES = -(-COLS // PIECE)
 UNITS = 2 * PIECES
 CHUNKS = 4
-GATE = 32
-RATE = {"x+": 46e3, "x-": 46e3, "z+": 46e3, "z-": 46e3, "y": 23e3}
+GATE = 36
+RATE = {"x+": 70e3, "x-": 70e3, "z+": 70e3, "z-": 70e3, "y": 60e3}
 
 
 def plan(rows_a, latency=1.7):
@@ -169,11 +169,13 @@
         for zz, p, go, a, base, (start, n) in units(tag):
             b = top.at[pl.ds(p * PIECE + start, n)]
             yield go, pltpu.make_async_copy(a, b, tl.at[base + p]), False
+            early = abs(tag[1]) <= 1
             if tag[2] == 0:
-                yield jnp.logical_and(go, zz >= 1), remote(a, b, ts.at[base + p], tr.at[base + p], across[0]), True
+                if not early:
+                    yield go, remote(a, b, ts.at[base + p], tr.at[base + p], across[0]), True
                 yield go, remote(a, b, ts.at[UNITS + base + p], tr.at[base + p], across[1]), True
-            else:
-                yield jnp.logical_and(go, zz == 0), remote(a, b, ts.at[UNITS + base + p], tr.at[base + p], across[1]), True
+            elif early:
+                yield go, remote(a, b, ts.at[UNITS + base + p], tr.at[base + p], across[1]), True
 
     def hand_up(tag):
         for go, c, _ in copies(tag):

time: 94.5 us -> 94 us (level)
  no operation moved by 1% of the time
where the time goes in v5:
time: 94 us; the launch traced here: 93.9 us
  Pallas kernels  93.7 us (100%)
    pallas_call x1, Pallas kernels, local(): pl.pallas_call(gather_solve, out_shape=(jax.ShapeDtypeStruct((NZ, NH, NX,...  81 us
    pallas_call x1, Pallas kernels, local(): pl.pallas_call(update, out_shape=jax.ShapeDtypeStruct((rows, width), jnp....  12.7 us

profile of v5, /device:TPU:1, one launch (start us, length us, event | category | flops | bytes accessed | tf_op | source)
XLA Modules:
  0.0 93.9 jit_solution(4719011729773233323)
XLA Ops:
  0.0 81.0 %shard_map.28 = (f32[8,2,4,40,1024]{4,3,2,1,0:T(8,128)}, f32[1024,512]{1,0:T(8,128)}) custom-call(f32[40,1024]{1,0:T(8,128)} %f_ref.1, f32[2560,512]{1,0:T(8,128)} %r_ref.3), custom_call_target="tpu_custom_call" | custom-call | tf_op jit(solution)/shard_map/pallas_call | solution.py:353
  81.0 12.7 %shard_map.29 = f32[2560,512]{1,0:T(8,128)} custom-call(f32[2560,1024]{1,0:T(8,128)} %bitcast.1, f32[1024,512]{1,0:T(8,128)} %get-tuple-element.8.x_ref, f32[2560,512]{1,0:T(8,128)} %r_ref.3), custom_call_target="tpu_custom_call" | custom-call | tf_op jit(solution)/shard_map/pallas_call | solution.py:377
